TPU v7x, 32 devices: a whole 2x2x4 slice. The times are simulated.
32 devices in a mesh: seq: 8 (over z, x), head: 4 (over y, core).
Axes of the slice: x: 2, y: 2, z: 4, core: 2. Of those that a mesh axis runs over, the one named last changes fastest.
Arguments:
- queries: bfloat16 [2, 8, 14336], P(None, 'seq', 'head'), may hold values from -150 to 150
- new_keys: bfloat16 [2, 8, 14336], P(None, 'seq', 'head'), may hold values from -6 to 6
- new_values: bfloat16 [2, 8, 14336], P(None, 'seq', 'head'), may hold values from -6 to 6
- cache_keys: bfloat16 [8192, 14336], P('seq', 'head'), may hold values from -6 to 6
- cache_values: bfloat16 [8192, 14336], P('seq', 'head'), may hold values from -6 to 6
- slopes: float32 [112], P('head'), may hold values from 7.324219e-05 to 0.025
- seg_blocks: int32 [8], replicated, may hold values from 1 to 32, 48 in all
- request_row: int32 [8], replicated, may hold values from 0 to 7, each once
- out_weight: bfloat16 [14336, 14336], P('head', 'seq'), may hold values from -0.046875 to 0.046875
- residual: bfloat16 [2, 8, 14336], P(None, 'head', 'seq'), may hold values from -6 to 6
Outputs:
- mixed: bfloat16 [2, 8, 14336], P(None, 'head', 'seq')
Inputs may be any that keep to these rules, and one draw needn't show every extreme that they name: `seg_blocks`: the requests are packed in order from block 0; 48 blocks are used and the rest of the cache is unused. `request_row`: each query row belongs to exactly one request.
All inputs are finite; a program needn't handle non-finite values.
Results may differ from a plain program's by a relative error of at most 0.006.
Values may be sent and summed in bfloat16 or wider, within the bound.
A program may use at most 64 MiB of HBM per device.

v0:
```python
import math

import jax
import jax.numpy as jnp
from jax import lax
from jax.sharding import PartitionSpec as P

BLK = 128


NEG = -1e30


def combine(first, second):
    top_a, sum_a, acc_a = first
    top_b, sum_b, acc_b = second
    top = jnp.maximum(top_a, top_b)
    weight_a = jnp.exp(top_a - top)
    weight_b = jnp.exp(top_b - top)
    return (
        top,
        sum_a * weight_a + sum_b * weight_b,
        acc_a * weight_a[..., None] + acc_b * weight_b[..., None],
    )


def self_terms(query, key_new, value_new, slopes, scale):
    query = query.astype(jnp.float32)
    key_new = key_new.astype(jnp.float32)
    value_new = value_new.astype(jnp.float32)
    first = jnp.sum(query[0] * key_new[0], axis=-1) * scale
    cross = jnp.sum(query[1] * key_new[0], axis=-1) * scale - slopes
    second = jnp.sum(query[1] * key_new[1], axis=-1) * scale
    upper = jnp.maximum(cross, second)
    e_cross = jnp.exp(cross - upper)
    e_second = jnp.exp(second - upper)
    top = jnp.stack([first, upper])
    total = jnp.stack([jnp.ones_like(first), e_cross + e_second])
    acc = jnp.stack(
        [value_new[0], e_cross[..., None] * value_new[0] + e_second[..., None] * value_new[1]]
    )
    return (top, total, acc)


def body(
    queries,
    new_keys,
    new_values,
    cache_keys,
    cache_values,
    slopes,
    seg_blocks,
    request_row,
    out_weight,
    residual,
):
    heads = slopes.shape[0]
    width = queries.shape[2]
    hdim = width // heads
    requests = seg_blocks.shape[0]
    own_rows = queries.shape[1]
    blocks = cache_keys.shape[0] // BLK
    scale = 1.0 / math.sqrt(hdim)
    everyone = lax.all_gather(queries, "seq", axis=1, tiled=True)
    place = lax.axis_index("seq")
    starts = jnp.cumsum(seg_blocks) - seg_blocks
    index = place * blocks + jnp.arange(blocks, dtype=jnp.int32)
    hit = (index[:, None] >= starts[None, :]) & (index[:, None] < (starts + seg_blocks)[None, :])
    live = jnp.any(hit, axis=1)
    block_row = jnp.sum(jnp.where(hit, request_row[None, :], 0), axis=1)
    first = jnp.sum(jnp.where(hit, starts[None, :], 0), axis=1)
    length = jnp.sum(jnp.where(hit, seg_blocks[None, :], 0), axis=1)
    base = length * BLK - (index - first) * BLK
    block_query = jnp.take(everyone, block_row, axis=1).reshape(2, blocks, heads, hdim)
    keys = cache_keys.reshape(blocks, BLK, heads, hdim)
    values = cache_values.reshape(blocks, BLK, heads, hdim)
    scores = (
        jnp.einsum("sbhd,bthd->bsht", block_query, keys, preferred_element_type=jnp.float32) * scale
    )
    dist = (
        base[:, None, None]
        + jnp.arange(2, dtype=jnp.int32)[None, :, None]
        - jnp.arange(BLK, dtype=jnp.int32)[None, None, :]
    ).astype(jnp.float32)
    scores = scores - slopes[None, None, :, None] * dist[:, :, None, :]
    top = jnp.max(scores, axis=-1)
    probs = jnp.exp(scores - top[..., None])
    total = jnp.sum(probs, axis=-1)
    acc = jnp.einsum(
        "bsht,bthd->bshd", probs.astype(jnp.bfloat16), values, preferred_element_type=jnp.float32
    )
    top = jnp.where(live[:, None, None], top, NEG)
    total = jnp.where(live[:, None, None], total, 0.0)
    acc = jnp.where(live[:, None, None, None], acc, 0.0)
    rowhot = (block_row[:, None] == jnp.arange(requests, dtype=jnp.int32)[None, :]) & live[:, None]
    tab_top = jnp.max(jnp.where(rowhot[:, :, None, None], top[:, None], NEG), axis=0).transpose(
        1, 0, 2
    )
    ratio = jnp.exp(top - jnp.take(tab_top, block_row, axis=1).transpose(1, 0, 2))
    onehot = rowhot.astype(jnp.float32)
    tab_sum = jnp.einsum("br,bsh->srh", onehot, ratio * total, precision=lax.Precision.HIGHEST)
    tab_acc = jnp.einsum(
        "br,bshd->srhd", onehot, ratio[..., None] * acc, precision=lax.Precision.HIGHEST
    )
    mine = self_terms(
        queries.reshape(2, own_rows, heads, hdim),
        new_keys.reshape(2, own_rows, heads, hdim),
        new_values.reshape(2, own_rows, heads, hdim),
        slopes,
        scale,
    )
    got_top, got_sum, got_acc = (
        lax.all_to_all(tab_top[None], "seq", split_axis=2, concat_axis=0, tiled=True),
        lax.all_to_all(tab_sum[None], "seq", split_axis=2, concat_axis=0, tiled=True),
        lax.all_to_all(tab_acc[None], "seq", split_axis=2, concat_axis=0, tiled=True),
    )
    highest = jnp.max(got_top, axis=0)
    factor = jnp.exp(got_top - highest[None])
    gathered_sum = jnp.sum(got_sum * factor, axis=0)
    gathered_acc = jnp.sum(got_acc * factor[..., None], axis=0)
    top_own, sum_own, acc_own = combine((highest, gathered_sum, gathered_acc), mine)
    attended = (acc_own / sum_own[..., None]).astype(jnp.bfloat16).reshape(2, own_rows, width)
    projected = jnp.einsum(
        "srx,xy->sry",
        lax.all_gather(attended, "seq", axis=1, tiled=True),
        out_weight,
        preferred_element_type=jnp.float32,
    )
    summed = lax.psum_scatter(
        projected.astype(jnp.bfloat16), "head", scatter_dimension=1, tiled=True
    ).astype(jnp.float32)
    return (residual.astype(jnp.float32) + summed).astype(jnp.bfloat16)


def solution(mesh):
    in_specs = (
        P(None, "seq", "head"),
        P(None, "seq", "head"),
        P(None, "seq", "head"),
        P("seq", "head"),
        P("seq", "head"),
        P("head"),
        P(),
        P(),
        P("head", "seq"),
        P(None, "head", "seq"),
    )
    out_specs = P(None, "head", "seq")
    return jax.shard_map(body, mesh=mesh, in_specs=in_specs, out_specs=out_specs, check_vma=False)
```

profile of v0, /device:TPU:0, one launch (start us, length us, event | category | flops | bytes accessed | tf_op | source)
XLA Modules:
  0.0 161.4 jit_solution(8189962348176017590)
XLA Ops:
  0.0 0.8 reduce-window.8
  0.8 0.7 iota_add_fusion.1
  1.5 0.9 select_reduce_fusion.2
  2.6 32.6 %all_gather.6 = bf16[2,8,3584]{2,0,1:T(2,128)(2,1)S(1)} all-gather(bf16[2,1,3584]{2,0,1:T(2,128)(2,1)} %param.10), channel_id=1, replica_groups=mesh['seq'=8,'head'=4] {'seq'}, dimensions={1}, use_global_device_ids=true | all-gather | bytes 129024 | tf_op jit(solution)/shard_map/all_gather | solution.py:64
  35.4 12.9 %reshape.655 = bf16[8,128,28,128]{3,2,1,0:T(8,128)(2,1)} reshape(bf16[1024,3584]{1,0:T(8,128)(2,1)} %param.13) | data formatting | bytes 14680064 | tf_op jit(solution)/shard_map/reshape | solution.py:75
  48.3 0.8 gather_fusion
  49.2 7.4 %fusion.67 = (f32[8,2,28]{1,2,0:T(8,128)S(1)}, f32[8,2,28,128]{3,1,2,0:T(2,128)S(1)}) fusion(f32[8,2,128]{2,1,0:T(2,128)S(1)} %subtract_convert_fusion, f32[28]{0:T(128)S(1)} %copy-done.4, bf16[8,128,28,128]{3,2,1,0:T(8,128)(2,1)} %reshape.655, bf16[2,8,28,128]{3,1,2,0:T(8,128)(2,1)S(1)} %bitcast_select_fusion), kind=kOutput, calls=%fused_computation.103 | convolution fusion | flops 14908992 | bytes 7694192 | tf_op jit(solution)/shard_map/sbhd,bthd->bsht/dot_general | solution.py:78
  56.9 0.6 copy.210
  57.5 5.5 %all-to-all-start.1 = ((f32[1,2,8,28]{3,1,0,2:T(2,128)}), f32[1,2,8,28]{3,1,0,2:T(2,128)S(1)}, u32[]{:S(2)}, u32[]{:S(2)}) async-start(f32[1,2,8,28]{3,1,0,2:T(2,128)} %bitcast.107.clone.2), calls=%async_computation.1 | async-start | bytes 16384 | tf_op jit(solution)/shard_map/all_to_all | solution.py:113
  63.0 1.3 gather_fusion.1
  64.5 12.9 %reshape.656 = bf16[8,128,28,128]{3,2,1,0:T(8,128)(2,1)} reshape(bf16[1024,3584]{1,0:T(8,128)(2,1)} %param.14) | data formatting | bytes 14680064 | tf_op jit(solution)/shard_map/reshape | solution.py:76
  77.4 0.6 fusion.29
  78.0 6.6 %fusion.24 = f32[8,2,28,128]{3,1,2,0:T(2,128)S(1)} fusion(bf16[8,128,28,128]{3,2,1,0:T(8,128)(2,1)} %reshape.656, pred[8]{0:T(512)(128)(4,1)S(1)} %fusion.66, f32[8,2,28,128]{3,1,2,0:T(2,128)S(1)} %get-tuple-element.24, f32[8,2,28]{1,2,0:T(8,128)S(1)} %get-tuple-element.23, f32[8,2,28]{1,2,0:T(8,128)S(1)} %copy.154), kind=kOutput, calls=%fused_computation.16 | convolution fusion | flops 14909440 | bytes 7802376 | tf_op jit(solution)/shard_map/bsht,bthd->bshd/dot_general | solution.py:89
  85.8 0.9 copy.158
  86.7 0.6 copy.164
  87.3 0.6 dynamic-slice
  88.6 6.0 %all-to-all-start.2 = ((f32[1,2,8,28]{3,1,0,2:T(2,128)}), f32[1,2,8,28]{3,1,0,2:T(2,128)S(1)}, u32[]{:S(2)}, u32[]{:S(2)}) async-start(f32[1,2,8,28]{3,1,0,2:T(2,128)} %copy.164), calls=%async_computation.2 | async-start | bytes 16384 | tf_op jit(solution)/shard_map/all_to_all | solution.py:114
  94.8 6.4 %all-to-all-done.2 = f32[1,2,8,28]{3,1,0,2:T(2,128)S(1)} async-done(((f32[1,2,8,28]{3,1,0,2:T(2,128)}), f32[1,2,8,28]{3,1,0,2:T(2,128)S(1)}, u32[]{:S(2)}, u32[]{:S(2)}) %all-to-all-start.2) | async-done | bytes 1824 | tf_op jit(solution)/shard_map/all_to_all | solution.py:114
  101.2 3.4 %all-to-all-start = ((f32[1,2,8,28,128]{4,1,3,0,2:T(2,128)}), f32[1,2,8,28,128]{4,1,3,0,2:T(2,128)S(1)}, u32[]{:S(2)}, u32[]{:S(2)}) async-start(f32[1,2,8,28,128]{4,1,3,0,2:T(2,128)} %copy.158), calls=%async_computation | async-start | bytes 458752 | tf_op jit(solution)/shard_map/all_to_all | solution.py:115
  105.0 7.7 %all-to-all-done = f32[1,2,8,28,128]{4,1,3,0,2:T(2,128)S(1)} async-done(((f32[1,2,8,28,128]{4,1,3,0,2:T(2,128)}), f32[1,2,8,28,128]{4,1,3,0,2:T(2,128)S(1)}, u32[]{:S(2)}, u32[]{:S(2)}) %all-to-all-start) | async-done | bytes 229408 | tf_op jit(solution)/shard_map/all_to_all | solution.py:115
  113.1 30.6 %all_gather.7 = bf16[2,8,3584]{2,0,1:T(2,128)(2,1)S(1)} all-gather(bf16[2,1,3584]{2,0,1:T(2,128)(2,1)S(1)} %fusion.37), channel_id=1, replica_groups=mesh['seq'=8,'head'=4] {'seq'}, dimensions={1}, use_global_device_ids=true | all-gather | bytes 129024 | tf_op jit(solution)/shard_map/all_gather | solution.py:125
  143.6 6.4 %fusion.6 = bf16[2,8,1792]{2,1,0:T(8,128)(2,1)S(1)} fusion(bf16[3584,1792]{1,0:T(8,128)(2,1)} %param.18, bf16[2,8,3584]{2,0,1:T(2,128)(2,1)S(1)} %all_gather.7), kind=kOutput, calls=%fused_computation.8 | convolution fusion | flops 205549568 | bytes 13017088 | tf_op jit(solution)/shard_map/srx,xy->sry/dot_general | solution.py:123
  150.1 10.7 %all-reduce.1 = bf16[2,8,1792]{2,1,0:T(8,128)(2,1)S(1)} all-reduce(bf16[2,8,1792]{2,1,0:T(8,128)(2,1)S(1)} %fusion.6), channel_id=2, replica_groups=mesh['seq'=8,'head'=4] {'head'}, use_global_device_ids=true, to_apply=%region_14.15.clone | all-reduce | flops 28672 | bytes 114688
  160.8 0.6 add_convert_fusion
  (57 shorter events, 3.2 us)
Async XLA Ops:
  0.0 49.1 %copy-start.4 = (f32[28]{0:T(128)S(1)}, f32[28]{0:T(128)}, u32[]{:S(2)}) copy-start(f32[28]{0:T(128)} %param.15) | copy-start | bytes 340
  48.3 14.7 %copy-start.1 = (bf16[2,1,3584]{2,0,1:T(2,128)(2,1)S(1)}, bf16[2,1,3584]{2,0,1:T(2,128)(2,1)}, u32[]{:S(2)}) copy-start(bf16[2,1,3584]{2,0,1:T(2,128)(2,1)} %param.10) | copy-start | bytes 43012
  57.5 31.0 %all-to-all-start.1 = ((f32[1,2,8,28]{3,1,0,2:T(2,128)}), f32[1,2,8,28]{3,1,0,2:T(2,128)S(1)}, u32[]{:S(2)}, u32[]{:S(2)}) async-start(f32[1,2,8,28]{3,1,0,2:T(2,128)} %bitcast.107.clone.2), calls=%async_computation.1 | async-start | bytes 16384 | tf_op jit(solution)/shard_map/all_to_all | solution.py:113
  77.4 7.6 %copy-start.2 = (bf16[2,1,3584]{2,0,1:T(2,128)(2,1)S(1)}, bf16[2,1,3584]{2,0,1:T(2,128)(2,1)}, u32[]{:S(2)}) copy-start(bf16[2,1,3584]{2,0,1:T(2,128)(2,1)} %param.11) | copy-start | bytes 43012
  77.4 7.8 %copy-start = (bf16[2,1,3584]{2,0,1:T(2,128)(2,1)S(1)}, bf16[2,1,3584]{2,0,1:T(2,128)(2,1)}, u32[]{:S(2)}) copy-start(bf16[2,1,3584]{2,0,1:T(2,128)(2,1)} %param.12) | copy-start | bytes 43012
  77.4 9.9 %copy-start.5 = (u32[32]{0:T(128)S(1)}, u32[32]{0:T(128)}, u32[]{:S(2)}) copy-start(u32[32]{0:T(128)} %constant.63) | copy-start | bytes 388
  88.6 12.6 %all-to-all-start.2 = ((f32[1,2,8,28]{3,1,0,2:T(2,128)}), f32[1,2,8,28]{3,1,0,2:T(2,128)S(1)}, u32[]{:S(2)}, u32[]{:S(2)}) async-start(f32[1,2,8,28]{3,1,0,2:T(2,128)} %copy.164), calls=%async_computation.2 | async-start | bytes 16384 | tf_op jit(solution)/shard_map/all_to_all | solution.py:114
  94.8 66.0 %copy-start.3 = (bf16[2,2,1792]{2,1,0:T(2,128)(2,1)S(1)}, bf16[2,2,1792]{2,1,0:T(2,128)(2,1)}, u32[]{:S(2)}) copy-start(bf16[2,2,1792]{2,1,0:T(2,128)(2,1)} %param.19) | copy-start | bytes 43012
  101.2 11.4 %all-to-all-start = ((f32[1,2,8,28,128]{4,1,3,0,2:T(2,128)}), f32[1,2,8,28,128]{4,1,3,0,2:T(2,128)S(1)}, u32[]{:S(2)}, u32[]{:S(2)}) async-start(f32[1,2,8,28,128]{4,1,3,0,2:T(2,128)} %copy.158), calls=%async_computation | async-start | bytes 458752 | tf_op jit(solution)/shard_map/all_to_all | solution.py:115
where the time goes:
time: 163 us; the launch traced here: 161 us
  blocking collectives  73.9 us (45%)
  local copies, waits for them, and re-layouts  31.6 us (19%)
  matrix products  20.8 us (13%)
  starting transfers between devices  14.9 us (9%)
  waiting for transfers between devices  14.1 us (9%)
  other arithmetic  5.31 us (3%)
    all_gather x1, blocking collectives, body(): everyone = lax.all_gather(queries, 'seq', axis=1, tiled=True)  32.6 us
    all_gather x1, blocking collectives, body(): lax.all_gather(attended, 'seq', axis=1, tiled=True)  30.6 us
    reshape x1, local copies, waits for them, and re-layouts, body(): values = cache_values.reshape(blocks, BLK, heads, hdim)  12.9 us
    reshape x1, local copies, waits for them, and re-layouts, body(): keys = cache_keys.reshape(blocks, BLK, heads, hdim)  12.9 us
    unnamed x1, blocking collectives  10.7 us
    all_to_all x1, waiting for transfers between devices, body(): lax.all_to_all(tab_acc[None], 'seq', split_axis=2, concat_axis=0, tiled=T...  7.65 us
    dot_general x1, matrix products, body(): jnp.einsum('sbhd,bthd->bsht', block_query, keys, preferred_element_type=j...  7.37 us
    dot_general x1, matrix products, body(): jnp.einsum('bsht,bthd->bshd', probs.astype(jnp.bfloat16), values, preferr...  6.58 us
  transfers between devices with their start and end apart: 3, of which 2 were waited for; matrix products, arithmetic and copies ran while one was open for 16% of the time, Pallas kernels for 0%

commit v1 on v0

v1 whole, which is shorter than its diff:
```python
import functools
import math

import jax
import jax.numpy as jnp
from jax import lax
from jax.experimental import pallas as pl
from jax.experimental.pallas import tpu as pltpu
from jax.sharding import PartitionSpec as P

BLK = 128
FAR = 1e35
MESH = pl.DeviceIdType.MESH


def kernel(
    n_seq,
    n_head,
    heads,
    unit,
    tile,
    own_ref,
    seg_ref,
    row_ref,
    slope_ref,
    res_ref,
    k_hbm,
    v_hbm,
    w_hbm,
    out_ref,
    kbuf,
    vbuf,
    wbuf,
    qall,
    q2d,
    dist,
    o2d,
    st2d,
    sendb,
    recvb,
    attb,
    x_ref,
    shares,
    got,
    k_sem,
    v_sem,
    w_sem,
    q_send,
    q_recv,
    p_send,
    p_recv,
    a_send,
    a_recv,
    h_send,
    h_recv,
):
    hdim = own_ref.shape[3]
    rows = 2 * n_seq
    per = n_seq // n_head
    tokens = k_hbm.shape[0]
    padded = q2d.shape[0] // rows
    groups = heads // unit
    wide = unit * hdim
    cols = w_hbm.shape[1]
    scale = 1.0 / math.sqrt(hdim)
    me = lax.axis_index("seq")
    mine = lax.axis_index("head")

    def k_copy(g):
        at = pl.ds(pl.multiple_of(g * wide, 128), wide)
        return pltpu.make_async_copy(k_hbm.at[:, at], kbuf.at[:, at], k_sem.at[g])

    def v_copy(g):
        at = pl.ds(pl.multiple_of(g * wide, 128), wide)
        return pltpu.make_async_copy(v_hbm.at[:, at], vbuf.at[:, at], v_sem.at[g])

    def w_copy(g):
        at = pl.ds(pl.multiple_of(g * wide, 128), wide)
        return pltpu.make_async_copy(w_hbm.at[at], wbuf.at[at], w_sem.at[g])

    def to_seq(step):
        return lax.rem(me + step, n_seq)

    def to_head(step):
        return lax.rem(mine + step, n_head)

    barrier = pltpu.get_barrier_semaphore()
    for step in range(1, n_seq):
        pl.semaphore_signal(
            barrier, inc=1, device_id={"seq": to_seq(step)}, device_id_type=MESH
        )
    for step in range(1, n_head):
        pl.semaphore_signal(
            barrier, inc=1, device_id={"head": to_head(step)}, device_id_type=MESH
        )
    for g in range(groups):
        k_copy(g).start()
        v_copy(g).start()
    for g in range(groups):
        w_copy(g).start()
    pl.semaphore_wait(barrier, n_seq + n_head - 2)

    def q_copy(step):
        return pltpu.make_async_remote_copy(
            src_ref=own_ref.at[0],
            dst_ref=qall.at[me],
            send_sem=q_send.at[step - 1],
            recv_sem=q_recv.at[step - 1],
            device_id={"seq": to_seq(step)},
            device_id_type=MESH,
        )

    for step in range(1, n_seq):
        q_copy(step).start()

    line = lax.broadcasted_iota(jnp.int32, (rows, 1), 0)
    begin = jnp.zeros((rows, 1), jnp.int32)
    end = jnp.zeros((rows, 1), jnp.int32)
    at = jnp.int32(0)
    for i in range(n_seq):
        after = at + seg_ref[i]
        hit = (line // 2) == row_ref[i]
        begin = jnp.where(hit, at * BLK, begin)
        end = jnp.where(hit, after * BLK, end)
        at = after
    token = me * tokens + lax.broadcasted_iota(jnp.int32, (rows, tokens), 1)
    gap = (end + lax.rem(line, 2) - token).astype(jnp.float32)
    dist[...] = jnp.where((token >= begin) & (token < end), gap, FAR)

    lane = lax.broadcasted_iota(jnp.int32, (heads, hdim), 1)
    own = own_ref[...].astype(jnp.float32)
    slope_col = jnp.zeros((heads, 1), jnp.float32)
    hline = lax.broadcasted_iota(jnp.int32, (heads, 1), 0)
    for h in range(heads):
        slope_col = jnp.where(hline == h, slope_ref[h], slope_col)
    e00 = jnp.sum(own[0, 0] * own[1, 0], axis=-1, keepdims=True) * scale
    e10 = jnp.sum(own[0, 1] * own[1, 0], axis=-1, keepdims=True) * scale - slope_col
    e11 = jnp.sum(own[0, 1] * own[1, 1], axis=-1, keepdims=True) * scale
    upper = jnp.maximum(e10, e11)
    w10 = jnp.exp(e10 - upper)
    w11 = jnp.exp(e11 - upper)
    own_stat = jnp.where(
        lane == 0,
        e00,
        jnp.where(lane == 1, 1.0, jnp.where(lane == 2, upper, w10 + w11)),
    )
    own_acc = [own[2, 0], w10 * own[2, 0] + w11 * own[2, 1]]

    qall[me] = own_ref[0]
    for step in range(1, n_seq):
        q_copy(step).wait_recv()
    for r in range(n_seq):
        for s in range(2):
            q2d[pl.ds((2 * r + s) * padded, heads), :] = qall[r, s].astype(jnp.float32)

    odd = lax.rem(lax.broadcasted_iota(jnp.int32, (rows, hdim), 1), 2) == 1

    def attend(g, _):
        k_copy(g).wait()
        v_copy(g).wait()
        for u in range(unit):
            h = g * unit + u
            at = pl.ds(pl.multiple_of(h * hdim, 128), hdim)
            query = q2d[pl.ds(h, rows, stride=padded), :].astype(jnp.bfloat16)
            score = (
                lax.dot_general(
                    query,
                    kbuf[:, at],
                    (((1,), (1,)), ((), ())),
                    preferred_element_type=jnp.float32,
                )
                * scale
                - slope_ref[h] * dist[...]
            )
            top = jnp.max(score, axis=-1, keepdims=True)
            prob = jnp.exp(score - top)
            total = jnp.sum(prob, axis=-1, keepdims=True)
            put = pl.ds(pl.multiple_of(h * rows, 8), rows)
            o2d[put, :] = jnp.dot(
                prob.astype(jnp.bfloat16), vbuf[:, at], preferred_element_type=jnp.float32
            )
            st2d[put, :] = jnp.where(odd, total, top)
        return 0

    lax.fori_loop(0, groups, attend, 0)

    for r in range(n_seq):
        first = st2d[pl.ds(2 * r, heads, stride=rows), :]
        second = st2d[pl.ds(2 * r + 1, heads, stride=rows), :]
        stat = jnp.where(lax.rem(lane, 4) < 2, first, second)
        high = stat.astype(jnp.bfloat16).astype(jnp.float32)
        rest = stat - high
        middle = rest.astype(jnp.bfloat16).astype(jnp.float32)
        low = rest - middle
        sendb[r, 2] = jnp.where(lane < 4, high, jnp.where(lane < 8, middle, low)).astype(
            jnp.bfloat16
        )
        for s in range(2):
            sendb[r, s] = o2d[pl.ds(2 * r + s, heads, stride=rows), :].astype(jnp.bfloat16)

    def p_copy(step):
        return pltpu.make_async_remote_copy(
            src_ref=sendb.at[to_seq(step)],
            dst_ref=recvb.at[me],
            send_sem=p_send.at[step - 1],
            recv_sem=p_recv.at[step - 1],
            device_id={"seq": to_seq(step)},
            device_id_type=MESH,
        )

    for step in range(1, n_seq):
        p_copy(step).start()
    recvb[me] = sendb[me]
    for step in range(1, n_seq):
        p_copy(step).wait_recv()

    stats = [own_stat]
    for j in range(n_seq):
        x = recvb[j, 2].astype(jnp.float32)
        x = x + pltpu.roll(x, hdim - 4, 1) + pltpu.roll(x, hdim - 8, 1)
        stats.append(x)
    highest = functools.reduce(jnp.maximum, stats)
    factors = [jnp.exp(jnp.minimum(x - highest, 0.0)) for x in stats]
    total = sum(f * pltpu.roll(x, hdim - 1, 1) for f, x in zip(factors, stats))
    inverse = 1.0 / total
    pair = lax.div(me, per)
    place = lax.rem(me, per)
    for s in range(2):
        inv = inverse[:, 2 * s : 2 * s + 1]
        acc = factors[0][:, 2 * s : 2 * s + 1] * own_acc[s]
        for j in range(n_seq):
            acc += factors[j + 1][:, 2 * s : 2 * s + 1] * recvb[j, s].astype(jnp.float32)
        attb[pair, place, s] = (acc * inv).astype(jnp.bfloat16)

    def a_copy(step):
        return pltpu.make_async_remote_copy(
            src_ref=attb.at[pair, place],
            dst_ref=attb.at[pair, place],
            send_sem=a_send.at[step - 1],
            recv_sem=a_recv.at[step - 1],
            device_id={"seq": to_seq(step)},
            device_id_type=MESH,
        )

    def a_wait(step):
        source = lax.rem(me + n_seq - step, n_seq)
        here = attb.at[lax.div(source, per), lax.rem(source, per)]
        return pltpu.make_async_remote_copy(
            src_ref=here,
            dst_ref=here,
            send_sem=a_send.at[step - 1],
            recv_sem=a_recv.at[step - 1],
            device_id={"seq": to_seq(step)},
            device_id_type=MESH,
        )

    for step in range(1, n_seq):
        a_copy(step).start()
    for g in range(groups):
        w_copy(g).wait()
    for step in range(1, n_seq):
        a_wait(step).wait_recv()
    for k in range(n_head):
        for s in range(2):
            for j in range(per):
                n = (k * 2 + s) * per + j
                q2d[pl.ds(n * padded, heads), :] = attb[k, j, s].astype(jnp.float32)
    for h in range(heads):
        x_ref[:, h * hdim : (h + 1) * hdim] = q2d[pl.ds(h, rows, stride=padded), :].astype(
            jnp.bfloat16
        )

    for c in range(cols // tile):
        at = slice(c * tile, (c + 1) * tile)
        part = jnp.dot(x_ref[...], wbuf[:, at], preferred_element_type=jnp.float32)
        for k in range(n_head):
            shares[k, :, at] = part[2 * per * k : 2 * per * (k + 1)].astype(jnp.bfloat16)

    def h_copy(step):
        return pltpu.make_async_remote_copy(
            src_ref=shares.at[to_head(step)],
            dst_ref=got.at[step - 1],
            send_sem=h_send.at[step - 1],
            recv_sem=h_recv.at[step - 1],
            device_id={"head": to_head(step)},
            device_id_type=MESH,
        )

    for step in range(1, n_head):
        h_copy(step).start()
    summed = shares[mine].astype(jnp.float32)
    for step in range(1, n_head):
        h_copy(step).wait_recv()
        summed += got[step - 1].astype(jnp.float32)
    for s in range(2):
        out_ref[s] = (
            res_ref[s].astype(jnp.float32) + summed[s * per : (s + 1) * per]
        ).astype(jnp.bfloat16)
    for step in range(1, n_seq):
        q_copy(step).wait_send()
        p_copy(step).wait_send()
        a_copy(step).wait_send()
    for step in range(1, n_head):
        h_copy(step).wait_send()


def body(
    n_seq,
    n_head,
    queries,
    new_keys,
    new_values,
    cache_keys,
    cache_values,
    slopes,
    seg_blocks,
    request_row,
    out_weight,
    residual,
):
    heads = slopes.shape[0]
    width = queries.shape[2]
    hdim = width // heads
    tokens = cache_keys.shape[0]
    cols = out_weight.shape[1]
    assert queries.shape[1] == 1 and seg_blocks.shape[0] == n_seq
    own = jnp.stack([queries, new_keys, new_values]).reshape(3, 2, heads, hdim)
    unit = max(u for u in (1, 2, 4) if heads % u == 0)
    tile = 256 if cols % 256 == 0 else cols
    rows = 2 * n_seq
    per = n_seq // n_head
    padded = -(-heads // 8) * 8
    groups = heads // unit
    bf16, f32 = jnp.bfloat16, jnp.float32
    dma = pltpu.SemaphoreType.DMA
    vmem = pl.BlockSpec(memory_space=pltpu.VMEM)
    smem = pl.BlockSpec(memory_space=pltpu.SMEM)
    hbm = pl.BlockSpec(memory_space=pl.ANY)
    return pl.pallas_call(
        functools.partial(kernel, n_seq, n_head, heads, unit, tile),
        out_shape=jax.ShapeDtypeStruct(residual.shape, residual.dtype),
        in_specs=[vmem, smem, smem, smem, vmem, hbm, hbm, hbm],
        out_specs=vmem,
        scratch_shapes=[
            pltpu.VMEM(cache_keys.shape, bf16),
            pltpu.VMEM(cache_values.shape, bf16),
            pltpu.VMEM(out_weight.shape, bf16),
            pltpu.VMEM((n_seq, 2, heads, hdim), bf16),
            pltpu.VMEM((rows * padded, hdim), f32),
            pltpu.VMEM((rows, tokens), f32),
            pltpu.VMEM((heads * rows, hdim), f32),
            pltpu.VMEM((heads * rows, hdim), f32),
            pltpu.VMEM((n_seq, 3, heads, hdim), bf16),
            pltpu.VMEM((n_seq, 3, heads, hdim), bf16),
            pltpu.VMEM((n_head, per, 2, heads, hdim), bf16),
            pltpu.VMEM((rows, width), bf16),
            pltpu.VMEM((n_head, 2 * per, cols), bf16),
            pltpu.VMEM((n_head - 1, 2 * per, cols), bf16),
            dma((groups,)),
            dma((groups,)),
            dma((groups,)),
            dma((n_seq - 1,)),
            dma((n_seq - 1,)),
            dma((n_seq - 1,)),
            dma((n_seq - 1,)),
            dma((n_seq - 1,)),
            dma((n_seq - 1,)),
            dma((n_head - 1,)),
            dma((n_head - 1,)),
        ],
        compiler_params=pltpu.CompilerParams(
            collective_id=0, has_side_effects=True, vmem_limit_bytes=56 << 20
        ),
    )(own, seg_blocks, request_row, slopes, residual, cache_keys, cache_values, out_weight)


def solution(mesh):
    in_specs = (
        P(None, "seq", "head"),
        P(None, "seq", "head"),
        P(None, "seq", "head"),
        P("seq", "head"),
        P("seq", "head"),
        P("head"),
        P(),
        P(),
        P("head", "seq"),
        P(None, "head", "seq"),
    )
    out_specs = P(None, "head", "seq")
    sizes = (mesh.shape["seq"], mesh.shape["head"])
    return jax.shard_map(
        functools.partial(body, *sizes),
        mesh=mesh,
        in_specs=in_specs,
        out_specs=out_specs,
        check_vma=False,
    )
```

time: 163 us -> 41.7 us (0.26)
  blocking collectives: 73.9 us -> 0 us
  Pallas kernels: 0 us -> 37 us
  local copies, waits for them, and re-layouts: 31.6 us -> 3.52 us
  matrix products: 20.8 us -> 0 us
  starting transfers between devices: 14.9 us -> 0 us
  waiting for transfers between devices: 14.1 us -> 0 us
  other arithmetic: 5.31 us -> 0.63 us
    all_gather x2 -> x0, blocking collectives: 63.2 us -> none  [the longest x1 32.6 us: body(): everyone = lax.all_gather(queries, 'seq', axis=1, tiled=True)]
    pallas_call x0 -> x1, Pallas kernels: none -> 37 us  [body(): pl.pallas_call(functools.partial(kernel, n_seq, n_head, heads, unit, tile...]
    reshape x2 -> x0, local copies, waits for them, and re-layouts: 25.8 us -> none  [the longest x1 12.9 us: body(): values = cache_values.reshape(blocks, BLK, heads, hdim)]
    dot_general x5 -> x0, matrix products: 20.8 us -> none  [the longest x1 7.37 us: body(): jnp.einsum('sbhd,bthd->bsht', block_query, keys, preferred_element_type=j...]
    all_to_all x3 -> x0, starting transfers between devices: 14.9 us -> none  [the longest x1 6.01 us: body(): lax.all_to_all(tab_sum[None], 'seq', split_axis=2, concat_axis=0, tiled=T...]
    all_to_all x3 -> x0, waiting for transfers between devices: 14.1 us -> none  [the longest x1 7.65 us: body(): lax.all_to_all(tab_acc[None], 'seq', split_axis=2, concat_axis=0, tiled=T...]
    unnamed x1 -> x0, blocking collectives: 10.7 us -> none
    another operation x1 -> x3, local copies, waits for them, and re-layouts: 0.02 us -> 2.2 us  [body(): own = jnp.stack([queries, new_keys, new_values]).reshape(3, 2, heads, hdim)]
  transfers between devices with their start and end apart: 3 -> 0, of which waited for: 2 -> 0; matrix products, arithmetic and copies ran while one was open for 16% -> 0% of each run, Pallas kernels for 0% -> 0%
where the time goes in v1:
time: 41.7 us; the launch traced here: 41.2 us
  Pallas kernels  37 us (89%)
  local copies, waits for them, and re-layouts  3.52 us (8%)
  other arithmetic  0.63 us (2%)
    pallas_call x1, Pallas kernels, body(): pl.pallas_call(functools.partial(kernel, n_seq, n_head, heads, unit, tile...  37 us
    another operation x3, local copies, waits for them, and re-layouts, body(): own = jnp.stack([queries, new_keys, new_values]).reshape(3, 2, heads, hdim)  2.2 us
    unnamed x1, local copies, waits for them, and re-layouts  1.32 us

profile of v1, /device:TPU:0, one launch (start us, length us, event | category | flops | bytes accessed | tf_op | source)
XLA Modules:
  0.0 41.2 jit_solution(4958267505911788137)
XLA Ops:
  0.0 0.7 %stack.12 = bf16[1,2,28,128]{3,2,1,0:T(8,128)(2,1)S(1)} reshape(bf16[2,1,3584]{2,0,1:T(2,128)(2,1)} %param.10) | data formatting | bytes 28672 | tf_op jit(solution)/shard_map/stack | solution.py:327
  0.7 0.7 %stack.13 = bf16[1,2,28,128]{3,2,1,0:T(8,128)(2,1)S(1)} reshape(bf16[2,1,3584]{2,0,1:T(2,128)(2,1)} %param.11) | data formatting | bytes 28672 | tf_op jit(solution)/shard_map/stack | solution.py:327
  1.5 0.7 %stack.14 = bf16[1,2,28,128]{3,2,1,0:T(8,128)(2,1)S(1)} reshape(bf16[2,1,3584]{2,0,1:T(2,128)(2,1)} %param.12) | data formatting | bytes 28672 | tf_op jit(solution)/shard_map/stack | solution.py:327
  2.2 0.6 %pad_maximum_fusion.own_ref = bf16[3,2,28,128]{3,2,1,0:T(8,128)(2,1)} fusion(bf16[1,2,28,128]{3,2,1,0:T(8,128)(2,1)S(1)} %stack.14, bf16[1,2,28,128]{3,2,1,0:T(8,128)(2,1)S(1)} %stack.13, bf16[1,2,28,128]{3,2,1,0:T(8,128)(2,1)S(1)} %stack.12), kind=kLoop, calls=%fused_computation | loop fusion | flops 43008 | bytes 86016 | tf_op jit(solution)/shard_map/stack | solution.py:327
  2.8 37.0 %shard_map.100 = bf16[2,2,1792]{2,1,0:T(2,128)(2,1)} custom-call(bf16[3,2,28,128]{3,2,1,0:T(8,128)(2,1)} %pad_maximum_fusion.own_ref, s32[8]{0:T(128)} %seg_ref.1, s32[8]{0:T(128)} %row_ref.1, f32[28]{0:T(128)} %slope_ref.1, bf16[2,2,1792]{2,1,0:T(2,128)(2,1)} %res_ref.1, bf16[1024,3584]{1,0:T(8,128)(2,1)} %k_hbm.1, bf16[1024,3584]{1,0:T(8,128)(2,1)} %v_hbm.1, ...), custom_call_target="tpu_custom_call" | custom-call | tf_op jit(solution)/shard_map/pallas_call | solution.py:339
  39.8 1.3 %copy.12 = bf16[2,2,1792]{2,1,0:T(2,128)(2,1)} copy(bf16[2,2,1792]{2,1,0:T(2,128)(2,1)} %shard_map.100) | data formatting | bytes 28672

commit v2 on v1

--- a/solution.py
+++ b/solution.py
@@ -10,6 +10,7 @@
 
 BLK = 128
 FAR = 1e35
+LAG = 3
 MESH = pl.DeviceIdType.MESH
 
 
@@ -19,7 +20,9 @@
     heads,
     unit,
     tile,
-    own_ref,
+    qry_ref,
+    key_ref,
+    val_ref,
     seg_ref,
     row_ref,
     slope_ref,
@@ -32,6 +35,10 @@
     vbuf,
     wbuf,
     qall,
+    own2d,
+    qx,
+    sbuf,
+    pbuf,
     q2d,
     dist,
     o2d,
@@ -54,7 +61,7 @@
     h_send,
     h_recv,
 ):
-    hdim = own_ref.shape[3]
+    hdim = qry_ref.shape[1] // heads
     rows = 2 * n_seq
     per = n_seq // n_head
     tokens = k_hbm.shape[0]
@@ -102,7 +109,7 @@
 
     def q_copy(step):
         return pltpu.make_async_remote_copy(
-            src_ref=own_ref.at[0],
+            src_ref=qry_ref,
             dst_ref=qall.at[me],
             send_sem=q_send.at[step - 1],
             recv_sem=q_recv.at[step - 1],
@@ -128,14 +135,19 @@
     dist[...] = jnp.where((token >= begin) & (token < end), gap, FAR)
 
     lane = lax.broadcasted_iota(jnp.int32, (heads, hdim), 1)
-    own = own_ref[...].astype(jnp.float32)
+    for n, ref in enumerate((qry_ref, key_ref, val_ref)):
+        for h in range(heads):
+            own2d[n, 2 * h : 2 * h + 2, :] = ref[:, h * hdim : (h + 1) * hdim].astype(jnp.float32)
+    own = [
+        [own2d.at[n][pl.ds(t, heads, stride=2), :] for t in range(2)] for n in range(3)
+    ]
     slope_col = jnp.zeros((heads, 1), jnp.float32)
     hline = lax.broadcasted_iota(jnp.int32, (heads, 1), 0)
     for h in range(heads):
         slope_col = jnp.where(hline == h, slope_ref[h], slope_col)
-    e00 = jnp.sum(own[0, 0] * own[1, 0], axis=-1, keepdims=True) * scale
-    e10 = jnp.sum(own[0, 1] * own[1, 0], axis=-1, keepdims=True) * scale - slope_col
-    e11 = jnp.sum(own[0, 1] * own[1, 1], axis=-1, keepdims=True) * scale
+    e00 = jnp.sum(own[0][0] * own[1][0], axis=-1, keepdims=True) * scale
+    e10 = jnp.sum(own[0][1] * own[1][0], axis=-1, keepdims=True) * scale - slope_col
+    e11 = jnp.sum(own[0][1] * own[1][1], axis=-1, keepdims=True) * scale
     upper = jnp.maximum(e10, e11)
     w10 = jnp.exp(e10 - upper)
     w11 = jnp.exp(e11 - upper)
@@ -144,45 +156,55 @@
         e00,
         jnp.where(lane == 1, 1.0, jnp.where(lane == 2, upper, w10 + w11)),
     )
-    own_acc = [own[2, 0], w10 * own[2, 0] + w11 * own[2, 1]]
-
-    qall[me] = own_ref[0]
+    own_acc = [own[2][0], w10 * own[2][0] + w11 * own[2][1]]
+
+    qall[me] = qry_ref[...]
     for step in range(1, n_seq):
         q_copy(step).wait_recv()
     for r in range(n_seq):
-        for s in range(2):
-            q2d[pl.ds((2 * r + s) * padded, heads), :] = qall[r, s].astype(jnp.float32)
+        qx[2 * r : 2 * r + 2, :] = qall[r].astype(jnp.float32)
 
     odd = lax.rem(lax.broadcasted_iota(jnp.int32, (rows, hdim), 1), 2) == 1
 
-    def attend(g, _):
-        k_copy(g).wait()
-        v_copy(g).wait()
-        for u in range(unit):
-            h = g * unit + u
-            at = pl.ds(pl.multiple_of(h * hdim, 128), hdim)
-            query = q2d[pl.ds(h, rows, stride=padded), :].astype(jnp.bfloat16)
-            score = (
-                lax.dot_general(
-                    query,
-                    kbuf[:, at],
-                    (((1,), (1,)), ((), ())),
-                    preferred_element_type=jnp.float32,
-                )
-                * scale
-                - slope_ref[h] * dist[...]
-            )
-            top = jnp.max(score, axis=-1, keepdims=True)
-            prob = jnp.exp(score - top)
-            total = jnp.sum(prob, axis=-1, keepdims=True)
-            put = pl.ds(pl.multiple_of(h * rows, 8), rows)
-            o2d[put, :] = jnp.dot(
-                prob.astype(jnp.bfloat16), vbuf[:, at], preferred_element_type=jnp.float32
-            )
-            st2d[put, :] = jnp.where(odd, total, top)
-        return 0
-
-    lax.fori_loop(0, groups, attend, 0)
+    def lanes(h):
+        return slice(h * hdim, (h + 1) * hdim)
+
+    def lines(h):
+        return slice(h * rows, (h + 1) * rows)
+
+    def scores(h):
+        if h % unit == 0:
+            k_copy(h // unit).wait()
+        dots = lax.dot_general(
+            qx[:, lanes(h)].astype(jnp.bfloat16),
+            kbuf[:, lanes(h)],
+            (((1,), (1,)), ((), ())),
+            preferred_element_type=jnp.float32,
+        )
+        sbuf[lines(h), :] = dots * scale - slope_ref[h] * dist[...]
+
+    def soften(h):
+        score = sbuf[lines(h), :]
+        top = jnp.max(score, axis=-1, keepdims=True)
+        prob = jnp.exp(score - top)
+        total = jnp.sum(prob, axis=-1, keepdims=True)
+        pbuf[lines(h), :] = prob.astype(jnp.bfloat16)
+        st2d[lines(h), :] = jnp.where(odd, total, top)
+
+    def weigh(h):
+        if h % unit == 0:
+            v_copy(h // unit).wait()
+        o2d[lines(h), :] = jnp.dot(
+            pbuf[lines(h), :], vbuf[:, lanes(h)], preferred_element_type=jnp.float32
+        )
+
+    for h in range(heads + 2 * LAG):
+        if h < heads:
+            scores(h)
+        if 0 <= h - LAG < heads:
+            soften(h - LAG)
+        if 0 <= h - 2 * LAG:
+            weigh(h - 2 * LAG)
 
     for r in range(n_seq):
         first = st2d[pl.ds(2 * r, heads, stride=rows), :]
@@ -324,7 +346,7 @@
     tokens = cache_keys.shape[0]
     cols = out_weight.shape[1]
     assert queries.shape[1] == 1 and seg_blocks.shape[0] == n_seq
-    own = jnp.stack([queries, new_keys, new_values]).reshape(3, 2, heads, hdim)
+    flat = [x.reshape(2, width) for x in (queries, new_keys, new_values)]
     unit = max(u for u in (1, 2, 4) if heads % u == 0)
     tile = 256 if cols % 256 == 0 else cols
     rows = 2 * n_seq
@@ -339,13 +361,17 @@
     return pl.pallas_call(
         functools.partial(kernel, n_seq, n_head, heads, unit, tile),
         out_shape=jax.ShapeDtypeStruct(residual.shape, residual.dtype),
-        in_specs=[vmem, smem, smem, smem, vmem, hbm, hbm, hbm],
+        in_specs=[vmem, vmem, vmem, smem, smem, smem, vmem, hbm, hbm, hbm],
         out_specs=vmem,
         scratch_shapes=[
             pltpu.VMEM(cache_keys.shape, bf16),
             pltpu.VMEM(cache_values.shape, bf16),
             pltpu.VMEM(out_weight.shape, bf16),
-            pltpu.VMEM((n_seq, 2, heads, hdim), bf16),
+            pltpu.VMEM((n_seq, 2, width), bf16),
+            pltpu.VMEM((3, 2 * heads, hdim), f32),
+            pltpu.VMEM((rows, width), f32),
+            pltpu.VMEM((heads * rows, tokens), f32),
+            pltpu.VMEM((heads * rows, tokens), bf16),
             pltpu.VMEM((rows * padded, hdim), f32),
             pltpu.VMEM((rows, tokens), f32),
             pltpu.VMEM((heads * rows, hdim), f32),
@@ -371,7 +397,7 @@
         compiler_params=pltpu.CompilerParams(
             collective_id=0, has_side_effects=True, vmem_limit_bytes=56 << 20
         ),
-    )(own, seg_blocks, request_row, slopes, residual, cache_keys, cache_values, out_weight)
+    )(*flat, seg_blocks, request_row, slopes, residual, cache_keys, cache_values, out_weight)
 
 
 def solution(mesh):

time: 41.7 us -> 34.1 us (0.82)
  Pallas kernels: 37 us -> 32.4 us
  local copies, waits for them, and re-layouts: 3.52 us -> 1.32 us
  other arithmetic: 0.63 us -> 0 us
    pallas_call x1, Pallas kernels: 37 us -> 32.4 us  [body(): pl.pallas_call(functools.partial(kernel, n_seq, n_head, heads, unit, tile...]
    another operation x3 -> x0, local copies, waits for them, and re-layouts: 2.2 us -> none  [body(): own = jnp.stack([queries, new_keys, new_values]).reshape(3, 2, heads, hdim)]
    another operation x1 -> x0, other arithmetic: 0.63 us -> none  [body(): own = jnp.stack([queries, new_keys, new_values]).reshape(3, 2, heads, hdim)]
where the time goes in v2:
time: 34.1 us; the launch traced here: 33.7 us
  Pallas kernels  32.4 us (95%)
  local copies, waits for them, and re-layouts  1.32 us (4%)
    pallas_call x1, Pallas kernels, body(): pl.pallas_call(functools.partial(kernel, n_seq, n_head, heads, unit, tile...  32.4 us
    unnamed x1, local copies, waits for them, and re-layouts  1.32 us

profile of v2, /device:TPU:0, one launch (start us, length us, event | category | flops | bytes accessed | tf_op | source)
XLA Modules:
  0.0 33.7 jit_solution(17275639483863753794)
XLA Ops:
  0.0 32.4 %shard_map.100 = bf16[2,2,1792]{2,1,0:T(2,128)(2,1)} custom-call(bf16[2,3584]{1,0:T(2,128)(2,1)} %bitcast.3, bf16[2,3584]{1,0:T(2,128)(2,1)} %bitcast.4, bf16[2,3584]{1,0:T(2,128)(2,1)} %bitcast.5, s32[8]{0:T(128)} %seg_ref.1, s32[8]{0:T(128)} %row_ref.1, f32[28]{0:T(128)} %slope_ref.1, bf16[2,2,1792]{2,1,0:T(2,128)(2,1)} %res_ref.1, ...), custom_call_target="tpu_custom_call" | custom-call | tf_op jit(solution)/shard_map/pallas_call | solution.py:361
  32.4 1.3 %copy.12 = bf16[2,2,1792]{2,1,0:T(2,128)(2,1)} copy(bf16[2,2,1792]{2,1,0:T(2,128)(2,1)} %shard_map.100) | data formatting | bytes 28672

commit v3 on v2

--- a/solution.py
+++ b/solution.py
@@ -11,6 +11,7 @@
 BLK = 128
 FAR = 1e35
 LAG = 3
+PARTS = 2
 MESH = pl.DeviceIdType.MESH
 
 
@@ -47,6 +48,7 @@
     recvb,
     attb,
     x_ref,
+    sofar,
     shares,
     got,
     k_sem,
@@ -67,6 +69,8 @@
     tokens = k_hbm.shape[0]
     padded = q2d.shape[0] // rows
     groups = heads // unit
+    some = heads // PARTS
+    slot = padded // PARTS
     wide = unit * hdim
     cols = w_hbm.shape[1]
     scale = 1.0 / math.sqrt(hdim)
@@ -134,29 +138,34 @@
     gap = (end + lax.rem(line, 2) - token).astype(jnp.float32)
     dist[...] = jnp.where((token >= begin) & (token < end), gap, FAR)
 
-    lane = lax.broadcasted_iota(jnp.int32, (heads, hdim), 1)
+    lane = lax.broadcasted_iota(jnp.int32, (some, hdim), 1)
+    hline = lax.broadcasted_iota(jnp.int32, (some, 1), 0)
     for n, ref in enumerate((qry_ref, key_ref, val_ref)):
         for h in range(heads):
             own2d[n, 2 * h : 2 * h + 2, :] = ref[:, h * hdim : (h + 1) * hdim].astype(jnp.float32)
-    own = [
-        [own2d.at[n][pl.ds(t, heads, stride=2), :] for t in range(2)] for n in range(3)
-    ]
-    slope_col = jnp.zeros((heads, 1), jnp.float32)
-    hline = lax.broadcasted_iota(jnp.int32, (heads, 1), 0)
-    for h in range(heads):
-        slope_col = jnp.where(hline == h, slope_ref[h], slope_col)
-    e00 = jnp.sum(own[0][0] * own[1][0], axis=-1, keepdims=True) * scale
-    e10 = jnp.sum(own[0][1] * own[1][0], axis=-1, keepdims=True) * scale - slope_col
-    e11 = jnp.sum(own[0][1] * own[1][1], axis=-1, keepdims=True) * scale
-    upper = jnp.maximum(e10, e11)
-    w10 = jnp.exp(e10 - upper)
-    w11 = jnp.exp(e11 - upper)
-    own_stat = jnp.where(
-        lane == 0,
-        e00,
-        jnp.where(lane == 1, 1.0, jnp.where(lane == 2, upper, w10 + w11)),
-    )
-    own_acc = [own[2][0], w10 * own[2][0] + w11 * own[2][1]]
+
+    def own_terms(p):
+        own = [
+            [own2d.at[n][pl.ds(2 * p * some + t, some, stride=2), :] for t in range(2)]
+            for n in range(3)
+        ]
+        slope_col = jnp.zeros((some, 1), jnp.float32)
+        for h in range(some):
+            slope_col = jnp.where(hline == h, slope_ref[p * some + h], slope_col)
+        e00 = jnp.sum(own[0][0] * own[1][0], axis=-1, keepdims=True) * scale
+        e10 = jnp.sum(own[0][1] * own[1][0], axis=-1, keepdims=True) * scale - slope_col
+        e11 = jnp.sum(own[0][1] * own[1][1], axis=-1, keepdims=True) * scale
+        upper = jnp.maximum(e10, e11)
+        w10 = jnp.exp(e10 - upper)
+        w11 = jnp.exp(e11 - upper)
+        stat = jnp.where(
+            lane == 0,
+            e00,
+            jnp.where(lane == 1, 1.0, jnp.where(lane == 2, upper, w10 + w11)),
+        )
+        return stat, [own[2][0], w10 * own[2][0] + w11 * own[2][1]]
+
+    owned = [own_terms(p) for p in range(PARTS)]
 
     qall[me] = qry_ref[...]
     for step in range(1, n_seq):
@@ -198,6 +207,34 @@
             pbuf[lines(h), :], vbuf[:, lanes(h)], preferred_element_type=jnp.float32
         )
 
+    def message(p):
+        base = p * some * rows
+        for r in range(n_seq):
+            first = st2d[pl.ds(base + 2 * r, some, stride=rows), :]
+            second = st2d[pl.ds(base + 2 * r + 1, some, stride=rows), :]
+            stat = jnp.where(lax.rem(lane, 4) < 2, first, second)
+            high = stat.astype(jnp.bfloat16).astype(jnp.float32)
+            rest = stat - high
+            middle = rest.astype(jnp.bfloat16).astype(jnp.float32)
+            low = rest - middle
+            sendb[r, p, 2] = jnp.where(
+                lane < 4, high, jnp.where(lane < 8, middle, low)
+            ).astype(jnp.bfloat16)
+            for s in range(2):
+                sendb[r, p, s] = o2d[pl.ds(base + 2 * r + s, some, stride=rows), :].astype(
+                    jnp.bfloat16
+                )
+
+    def p_copy(p, step):
+        return pltpu.make_async_remote_copy(
+            src_ref=sendb.at[to_seq(step), p],
+            dst_ref=recvb.at[me, p],
+            send_sem=p_send.at[p, step - 1],
+            recv_sem=p_recv.at[p, step - 1],
+            device_id={"seq": to_seq(step)},
+            device_id_type=MESH,
+        )
+
     for h in range(heads + 2 * LAG):
         if h < heads:
             scores(h)
@@ -205,114 +242,108 @@
             soften(h - LAG)
         if 0 <= h - 2 * LAG:
             weigh(h - 2 * LAG)
-
-    for r in range(n_seq):
-        first = st2d[pl.ds(2 * r, heads, stride=rows), :]
-        second = st2d[pl.ds(2 * r + 1, heads, stride=rows), :]
-        stat = jnp.where(lax.rem(lane, 4) < 2, first, second)
-        high = stat.astype(jnp.bfloat16).astype(jnp.float32)
-        rest = stat - high
-        middle = rest.astype(jnp.bfloat16).astype(jnp.float32)
-        low = rest - middle
-        sendb[r, 2] = jnp.where(lane < 4, high, jnp.where(lane < 8, middle, low)).astype(
-            jnp.bfloat16
-        )
+        if h - 2 * LAG >= 0 and (h - 2 * LAG + 1) % some == 0:
+            p = (h - 2 * LAG) // some
+            message(p)
+            for step in range(1, n_seq):
+                p_copy(p, step).start()
+            recvb[me, p] = sendb[me, p]
+
+    pair = lax.div(me, per)
+    place = lax.rem(me, per)
+
+    def merge(p):
+        own_stat, own_acc = owned[p]
+        stats = [own_stat]
+        for j in range(n_seq):
+            x = recvb[j, p, 2].astype(jnp.float32)
+            x = x + pltpu.roll(x, hdim - 4, 1) + pltpu.roll(x, hdim - 8, 1)
+            stats.append(x)
+        highest = functools.reduce(jnp.maximum, stats)
+        factors = [jnp.exp(jnp.minimum(x - highest, 0.0)) for x in stats]
+        total = sum(f * pltpu.roll(x, hdim - 1, 1) for f, x in zip(factors, stats))
+        inverse = 1.0 / total
         for s in range(2):
-            sendb[r, s] = o2d[pl.ds(2 * r + s, heads, stride=rows), :].astype(jnp.bfloat16)
-
-    def p_copy(step):
+            inv = inverse[:, 2 * s : 2 * s + 1]
+            acc = factors[0][:, 2 * s : 2 * s + 1] * own_acc[s]
+            for j in range(n_seq):
+                acc += factors[j + 1][:, 2 * s : 2 * s + 1] * recvb[j, p, s].astype(jnp.float32)
+            attb[pair, place, p, s] = (acc * inv).astype(jnp.bfloat16)
+
+    def a_copy(p, step):
         return pltpu.make_async_remote_copy(
-            src_ref=sendb.at[to_seq(step)],
-            dst_ref=recvb.at[me],
-            send_sem=p_send.at[step - 1],
-            recv_sem=p_recv.at[step - 1],
+            src_ref=attb.at[pair, place, p],
+            dst_ref=attb.at[pair, place, p],
+            send_sem=a_send.at[p, step - 1],
+            recv_sem=a_recv.at[p, step - 1],
             device_id={"seq": to_seq(step)},
             device_id_type=MESH,
         )
 
-    for step in range(1, n_seq):
-        p_copy(step).start()
-    recvb[me] = sendb[me]
-    for step in range(1, n_seq):
-        p_copy(step).wait_recv()
-
-    stats = [own_stat]
-    for j in range(n_seq):
-        x = recvb[j, 2].astype(jnp.float32)
-        x = x + pltpu.roll(x, hdim - 4, 1) + pltpu.roll(x, hdim - 8, 1)
-        stats.append(x)
-    highest = functools.reduce(jnp.maximum, stats)
-    factors = [jnp.exp(jnp.minimum(x - highest, 0.0)) for x in stats]
-    total = sum(f * pltpu.roll(x, hdim - 1, 1) for f, x in zip(factors, stats))
-    inverse = 1.0 / total
-    pair = lax.div(me, per)
-    place = lax.rem(me, per)
-    for s in range(2):
-        inv = inverse[:, 2 * s : 2 * s + 1]
-        acc = factors[0][:, 2 * s : 2 * s + 1] * own_acc[s]
-        for j in range(n_seq):
-            acc += factors[j + 1][:, 2 * s : 2 * s + 1] * recvb[j, s].astype(jnp.float32)
-        attb[pair, place, s] = (acc * inv).astype(jnp.bfloat16)
-
-    def a_copy(step):
-        return pltpu.make_async_remote_copy(
-            src_ref=attb.at[pair, place],
-            dst_ref=attb.at[pair, place],
-            send_sem=a_send.at[step - 1],
-            recv_sem=a_recv.at[step - 1],
-            device_id={"seq": to_seq(step)},
-            device_id_type=MESH,
-        )
-
-    def a_wait(step):
+    def a_wait(p, step):
         source = lax.rem(me + n_seq - step, n_seq)
-        here = attb.at[lax.div(source, per), lax.rem(source, per)]
+        here = attb.at[lax.div(source, per), lax.rem(source, per), p]
         return pltpu.make_async_remote_copy(
             src_ref=here,
             dst_ref=here,
-            send_sem=a_send.at[step - 1],
-            recv_sem=a_recv.at[step - 1],
+            send_sem=a_send.at[p, step - 1],
+            recv_sem=a_recv.at[p, step - 1],
             device_id={"seq": to_seq(step)},
             device_id_type=MESH,
         )
 
-    for step in range(1, n_seq):
-        a_copy(step).start()
+    for p in range(PARTS):
+        for step in range(1, n_seq):
+            p_copy(p, step).wait_recv()
+        merge(p)
+        for step in range(1, n_seq):
+            a_copy(p, step).start()
     for g in range(groups):
         w_copy(g).wait()
-    for step in range(1, n_seq):
-        a_wait(step).wait_recv()
-    for k in range(n_head):
-        for s in range(2):
-            for j in range(per):
-                n = (k * 2 + s) * per + j
-                q2d[pl.ds(n * padded, heads), :] = attb[k, j, s].astype(jnp.float32)
-    for h in range(heads):
-        x_ref[:, h * hdim : (h + 1) * hdim] = q2d[pl.ds(h, rows, stride=padded), :].astype(
-            jnp.bfloat16
-        )
-
-    for c in range(cols // tile):
+
+    def h_copy(c, step):
         at = slice(c * tile, (c + 1) * tile)
-        part = jnp.dot(x_ref[...], wbuf[:, at], preferred_element_type=jnp.float32)
-        for k in range(n_head):
-            shares[k, :, at] = part[2 * per * k : 2 * per * (k + 1)].astype(jnp.bfloat16)
-
-    def h_copy(step):
         return pltpu.make_async_remote_copy(
-            src_ref=shares.at[to_head(step)],
-            dst_ref=got.at[step - 1],
-            send_sem=h_send.at[step - 1],
-            recv_sem=h_recv.at[step - 1],
+            src_ref=shares.at[to_head(step), :, at],
+            dst_ref=got.at[step - 1, :, at],
+            send_sem=h_send.at[c, step - 1],
+            recv_sem=h_recv.at[c, step - 1],
             device_id={"head": to_head(step)},
             device_id_type=MESH,
         )
 
-    for step in range(1, n_head):
-        h_copy(step).start()
+    for p in range(PARTS):
+        for step in range(1, n_seq):
+            a_wait(p, step).wait_recv()
+        for k in range(n_head):
+            for s in range(2):
+                for j in range(per):
+                    n = (k * 2 + s) * per + j
+                    q2d[pl.ds(n * padded + p * slot, some), :] = attb[k, j, p, s].astype(
+                        jnp.float32
+                    )
+        for h in range(some):
+            x_ref[:, lanes(p * some + h)] = q2d[
+                pl.ds(p * slot + h, rows, stride=padded), :
+            ].astype(jnp.bfloat16)
+        deep = slice(p * some * hdim, (p + 1) * some * hdim)
+        for c in range(cols // tile):
+            at = slice(c * tile, (c + 1) * tile)
+            part = jnp.dot(x_ref[:, deep], wbuf[deep, at], preferred_element_type=jnp.float32)
+            if p > 0:
+                part += sofar[:, at]
+            if p < PARTS - 1:
+                sofar[:, at] = part
+                continue
+            for k in range(n_head):
+                shares[k, :, at] = part[2 * per * k : 2 * per * (k + 1)].astype(jnp.bfloat16)
+            for step in range(1, n_head):
+                h_copy(c, step).start()
+
     summed = shares[mine].astype(jnp.float32)
     for step in range(1, n_head):
-        h_copy(step).wait_recv()
+        for c in range(cols // tile):
+            h_copy(c, step).wait_recv()
         summed += got[step - 1].astype(jnp.float32)
     for s in range(2):
         out_ref[s] = (
@@ -320,10 +351,12 @@
         ).astype(jnp.bfloat16)
     for step in range(1, n_seq):
         q_copy(step).wait_send()
-        p_copy(step).wait_send()
-        a_copy(step).wait_send()
+        for p in range(PARTS):
+            p_copy(p, step).wait_send()
+            a_copy(p, step).wait_send()
     for step in range(1, n_head):
-        h_copy(step).wait_send()
+        for c in range(cols // tile):
+            h_copy(c, step).wait_send()
 
 
 def body(
@@ -351,7 +384,9 @@
     tile = 256 if cols % 256 == 0 else cols
     rows = 2 * n_seq
     per = n_seq // n_head
-    padded = -(-heads // 8) * 8
+    some = heads // PARTS
+    padded = PARTS * (-(-some // 8) * 8)
+    assert heads % PARTS == 0
     groups = heads // unit
     bf16, f32 = jnp.bfloat16, jnp.float32
     dma = pltpu.SemaphoreType.DMA
@@ -376,10 +411,11 @@
             pltpu.VMEM((rows, tokens), f32),
             pltpu.VMEM((heads * rows, hdim), f32),
             pltpu.VMEM((heads * rows, hdim), f32),
-            pltpu.VMEM((n_seq, 3, heads, hdim), bf16),
-            pltpu.VMEM((n_seq, 3, heads, hdim), bf16),
-            pltpu.VMEM((n_head, per, 2, heads, hdim), bf16),
+            pltpu.VMEM((n_seq, PARTS, 3, some, hdim), bf16),
+            pltpu.VMEM((n_seq, PARTS, 3, some, hdim), bf16),
+            pltpu.VMEM((n_head, per, PARTS, 2, some, hdim), bf16),
             pltpu.VMEM((rows, width), bf16),
+            pltpu.VMEM((rows, cols), f32),
             pltpu.VMEM((n_head, 2 * per, cols), bf16),
             pltpu.VMEM((n_head - 1, 2 * per, cols), bf16),
             dma((groups,)),
@@ -387,12 +423,12 @@
             dma((groups,)),
             dma((n_seq - 1,)),
             dma((n_seq - 1,)),
-            dma((n_seq - 1,)),
-            dma((n_seq - 1,)),
-            dma((n_seq - 1,)),
-            dma((n_seq - 1,)),
-            dma((n_head - 1,)),
-            dma((n_head - 1,)),
+            dma((PARTS, n_seq - 1)),
+            dma((PARTS, n_seq - 1)),
+            dma((PARTS, n_seq - 1)),
+            dma((PARTS, n_seq - 1)),
+            dma((cols // tile, n_head - 1)),
+            dma((cols // tile, n_head - 1)),
         ],
         compiler_params=pltpu.CompilerParams(
             collective_id=0, has_side_effects=True, vmem_limit_bytes=56 << 20

time: 34.1 us -> 33.6 us (0.985)
  Pallas kernels: 32.4 us -> 31.9 us
    pallas_call x1, Pallas kernels: 32.4 us -> 31.9 us  [body(): pl.pallas_call(functools.partial(kernel, n_seq, n_head, heads, unit, tile...]
where the time goes in v3:
time: 33.6 us; the launch traced here: 33.2 us
  Pallas kernels  31.9 us (95%)
  local copies, waits for them, and re-layouts  1.32 us (4%)
    pallas_call x1, Pallas kernels, body(): pl.pallas_call(functools.partial(kernel, n_seq, n_head, heads, unit, tile...  31.9 us
    unnamed x1, local copies, waits for them, and re-layouts  1.32 us

profile of v3, /device:TPU:0, one launch (start us, length us, event | category | flops | bytes accessed | tf_op | source)
XLA Modules:
  0.0 33.2 jit_solution(2507496045471173926)
XLA Ops:
  0.0 31.9 %shard_map.100 = bf16[2,2,1792]{2,1,0:T(2,128)(2,1)} custom-call(bf16[2,3584]{1,0:T(2,128)(2,1)} %bitcast.3, bf16[2,3584]{1,0:T(2,128)(2,1)} %bitcast.4, bf16[2,3584]{1,0:T(2,128)(2,1)} %bitcast.5, s32[8]{0:T(128)} %seg_ref.1, s32[8]{0:T(128)} %row_ref.1, f32[28]{0:T(128)} %slope_ref.1, bf16[2,2,1792]{2,1,0:T(2,128)(2,1)} %res_ref.1, ...), custom_call_target="tpu_custom_call" | custom-call | tf_op jit(solution)/shard_map/pallas_call | solution.py:396
  31.9 1.3 %copy.12 = bf16[2,2,1792]{2,1,0:T(2,128)(2,1)} copy(bf16[2,2,1792]{2,1,0:T(2,128)(2,1)} %shard_map.100) | data formatting | bytes 28672
